TPU v7x, 32 devices: a whole 2x2x4 slice. The times are simulated.
32 devices in a mesh: gx: 8 (over y, x, core), gy: 4 (over z).
Axes of the slice: x: 2, y: 2, z: 4, core: 2. Of those that a mesh axis runs over, the one named last changes fastest.
Arguments:
- velocity: float32 [3, 1, 384, 1024], P(None, None, 'gy', 'gx'), may hold values from -6 to 6
- block_inverse: float32 [384, 96], P('gy'), may hold values from -1.6 to 1.6, as said below
- lower_map: float32 [384, 96], P('gy'), may hold values from -1 to 1
- upper_map: float32 [384, 96], P('gy'), may hold values from -1 to 1
Outputs:
- new_velocity: float32 [3, 1, 384, 2048], P(None, None, 'gy', 'gx')
Inputs may be any that keep to these rules, and one draw needn't show every extreme that they name: `block_inverse`: entries of the given block inverses.
All inputs are finite; a program needn't handle non-finite values.
Results may differ from a plain program's by a relative error of at most 0.00012.
Values sent between devices are 32-bit elements; how exact they have to be, the bound alone decides.
A program may use at most 64 MiB of HBM per device.

v0:
```python
import math

import jax
import jax.numpy as jnp
from jax import lax
from jax.sharding import PartitionSpec as P

courant = 0.8


def from_partner(shard, axis, bit):
    return lax.ppermute(shard, axis, [(i, i ^ 1 << bit) for i in range(lax.axis_size(axis))])


def reversed_position(position, levels):
    result = jnp.zeros((), jnp.int32)
    for digit_place in range(levels):
        result = result + (position >> digit_place & 1) * (1 << levels - 1 - digit_place)
    return result


def advance(matrix, state):
    return jnp.einsum("ab,spbw->spaw", matrix, state, precision=lax.Precision.HIGHEST)


def local_transform(paired, leading, count_gx, total_x):
    local_x = paired.shape[-1] // 2
    cells = jnp.arange(local_x, dtype=jnp.int32)
    wavenumbers = leading + count_gx * cells
    phases = cells[:, None] * wavenumbers[None, :] % total_x
    angles = 2.0 * math.pi / total_x * phases.astype(jnp.float32)
    cosine = jnp.cos(angles)
    sine_table = jnp.sin(angles)
    transform_matrix = jnp.concatenate(
        [jnp.concatenate([cosine, -sine_table], 1), jnp.concatenate([sine_table, cosine], 1)], 0
    )
    product = jnp.dot(
        paired,
        transform_matrix,
        precision=lax.Precision.HIGHEST,
        preferred_element_type=jnp.float32,
    )
    return product * (1.0 / math.sqrt(total_x))


def local_sweeps(lower_blocks, upper_blocks, loads):

    def step_once(state_prev, inputs):
        fresh = inputs[1] + advance(inputs[0], state_prev)
        return (fresh, fresh)

    start_state = jnp.zeros(loads.shape[1:], jnp.float32)
    unused, sweeps = lax.scan(step_once, start_state, (lower_blocks, loads))
    unused, solved = lax.scan(step_once, start_state, (upper_blocks, sweeps), reverse=True)
    return solved


def shards(velocity, block_inverse, lower_map, upper_map):
    fluxes = velocity[0:1] * velocity
    fields = jnp.concatenate([velocity, fluxes], 0)
    planes_here = fields.shape[1]
    rows_here = fields.shape[2]
    local_x = fields.shape[3]
    count_gx = lax.axis_size("gx")
    levels = count_gx.bit_length() - 1
    position = lax.axis_index("gx")
    total_x = local_x * count_gx
    current = jnp.stack([fields, jnp.zeros_like(fields)])
    for digit_place in reversed(range(levels)):
        half_span = 1 << digit_place
        if digit_place == levels - 1:
            real_partner = from_partner(fields, "gx", digit_place)
            partner = jnp.stack([real_partner, jnp.zeros_like(real_partner)])
        else:
            partner = from_partner(current, "gx", digit_place)
        is_upper = position >> digit_place & 1 == 1
        offset = (position & half_span - 1).astype(jnp.float32)
        angles = offset * (-math.pi / half_span)
        cosine = jnp.cos(angles)
        sine_value = jnp.sin(angles)
        diff_real = partner[0] - current[0]
        diff_imag = partner[1] - current[1]
        turned = jnp.stack(
            [
                diff_real * cosine - diff_imag * sine_value,
                diff_real * sine_value + diff_imag * cosine,
            ]
        )
        current = jnp.where(is_upper, turned, current + partner)
    paired = jnp.concatenate([current[0], current[1]], -1)
    leading = reversed_position(position, levels)
    spectra = local_transform(paired, leading, count_gx, total_x)
    velocity_modes = spectra[:3]
    flux_modes = spectra[3:]
    wavenumbers = leading + count_gx * jnp.arange(local_x, dtype=jnp.int32)
    signed = jnp.where(wavenumbers < total_x // 2, wavenumbers, wavenumbers - total_x)
    factor = courant * signed.astype(jnp.float32) / (total_x // 2)
    side_real = velocity_modes[..., :local_x] + factor * flux_modes[..., local_x:]
    side_imag = velocity_modes[..., local_x:] - factor * flux_modes[..., :local_x]
    right_side = jnp.concatenate([side_real, side_imag], -1)
    loads = advance(block_inverse, right_side)
    count_gy = lax.axis_size("gy")
    column_total = loads.shape[-1]
    column_count = column_total // count_gy
    lowers, uppers = (
        lax.all_gather(lower_map, "gy", axis=0, tiled=True),
        lax.all_gather(upper_map, "gy", axis=0, tiled=True),
    )
    lower_blocks = lowers.reshape(count_gy, rows_here, rows_here)
    upper_blocks = uppers.reshape(count_gy, rows_here, rows_here)
    grouped = loads.reshape(3, planes_here, rows_here, count_gy, column_count)
    profiles = lax.all_to_all(grouped, "gy", split_axis=3, concat_axis=2, tiled=True)
    items = profiles.shape[0]
    blocked = profiles.reshape(items, planes_here, count_gy, rows_here, column_count)
    blocked = jnp.moveaxis(blocked, 2, 0)
    solved_blocks = local_sweeps(lower_blocks, upper_blocks, blocked)
    whole = jnp.moveaxis(solved_blocks, 0, 2).reshape(
        items, planes_here, count_gy * rows_here, 1, column_count
    )
    finished = lax.all_to_all(whole, "gy", split_axis=2, concat_axis=3, tiled=True)
    solved = finished.reshape(3, planes_here, rows_here, column_total)
    return solved


def solution(mesh):
    return jax.shard_map(
        shards,
        mesh=mesh,
        in_specs=(P(None, None, "gy", "gx"), P("gy", None), P("gy", None), P("gy", None)),
        out_specs=P(None, None, "gy", "gx"),
        check_vma=False,
    )
```

profile of v0, /device:TPU:0, one launch (start us, length us, event | category | flops | bytes accessed | tf_op | source)
XLA Modules:
  0.0 91.6 jit_solution(16802690939830432598)
XLA Ops:
  0.0 0.8 slice_bitcast_fusion.2
  0.8 1.0 %broadcast_multiply_fusion = f32[3,1,96,128]{3,2,0,1:T(8,128)S(1)} fusion(f32[96,128]{1,0:T(8,128)S(1)} %slice_bitcast_fusion.2, f32[3,1,96,128]{3,2,1,0:T(8,128)} %param.8), kind=kLoop, calls=%fused_computation.53 | loop fusion | flops 36864 | bytes 344064 | tf_op jit(solution)/shard_map/mul | solution.py:59
  1.9 3.1 %collective-permute-start = (f32[6,1,96,128]{3,2,0,1:T(8,128)S(1)}, f32[6,1,96,128]{3,2,0,1:T(8,128)S(1)}, u32[]{:S(2)}, u32[]{:S(2)}) collective-permute-start(f32[6,1,96,128]{3,2,0,1:T(8,128)S(1)} %pad_maximum_fusion), channel_id=1, source_target_pairs={{0,16},{4,20},{8,24},{12,28},{16,0},{20,4},{24,8},{28,12},{1,17},{... | collective-permute-start | bytes 884744 | tf_op jit(solution)/shard_map/ppermute | solution.py:12
  5.1 6.8 %collective-permute-done = f32[6,1,96,128]{3,2,0,1:T(8,128)S(1)} collective-permute-done((f32[6,1,96,128]{3,2,0,1:T(8,128)S(1)}, f32[6,1,96,128]{3,2,0,1:T(8,128)S(1)}, u32[]{:S(2)}, u32[]{:S(2)}) %collective-permute-start) | collective-permute-done | bytes 294944 | tf_op jit(solution)/shard_map/ppermute | solution.py:12
  12.1 1.8 %collective-permute-start.1 = (f32[2,6,1,96,128]{4,3,1,2,0:T(8,128)S(1)}, f32[2,6,1,96,128]{4,3,1,2,0:T(8,128)S(1)}, u32[]{:S(2)}, u32[]{:S(2)}) collective-permute-start(f32[2,6,1,96,128]{4,3,1,2,0:T(8,128)S(1)} %maximum_select_fusion), channel_id=1, source_target_pairs={{0,8},{4,12},{8,0},{12,4},{16,24},{20,28},{24,16},{28,20},{1,9},{5... | collective-permute-start | bytes 1769480 | tf_op jit(solution)/shard_map/ppermute | solution.py:12
  14.0 12.6 %collective-permute-done.1 = f32[2,6,1,96,128]{4,3,1,2,0:T(8,128)S(1)} collective-permute-done((f32[2,6,1,96,128]{4,3,1,2,0:T(8,128)S(1)}, f32[2,6,1,96,128]{4,3,1,2,0:T(8,128)S(1)}, u32[]{:S(2)}, u32[]{:S(2)}) %collective-permute-start.1) | collective-permute-done | bytes 589856 | tf_op jit(solution)/shard_map/ppermute | solution.py:12
  27.0 0.3 fusion.30
  27.3 1.7 %collective-permute-done.2 = f32[2,6,1,96,128]{4,3,1,2,0:T(8,128)S(1)} collective-permute-done((f32[2,6,1,96,128]{4,3,1,2,0:T(8,128)S(1)}, f32[2,6,1,96,128]{4,3,1,2,0:T(8,128)S(1)}, u32[]{:S(2)}, u32[]{:S(2)}) %collective-permute-start.2) | collective-permute-done | bytes 589856 | tf_op jit(solution)/shard_map/ppermute | solution.py:12
  29.2 0.6 fusion.8
  29.9 0.4 convolution_bitcast_fusion
  30.5 0.8 copy.28
  31.2 4.9 %all-to-all-start = ((f32[3,1,96,4,64]{2,4,0,1,3:T(8,128)}), f32[3,1,96,4,64]{2,4,0,1,3:T(8,128)S(1)}, u32[]{:S(2)}, u32[]{:S(2)}) async-start(f32[3,1,96,4,64]{2,4,0,1,3:T(8,128)} %copy.28), calls=%async_computation | async-start | bytes 786432 | tf_op jit(solution)/shard_map/all_to_all | solution.py:112
  36.2 19.4 %all_gather.6 = f32[384,96]{1,0:T(8,128)S(1)} all-gather(f32[96,96]{1,0:T(8,128)S(1)} %copy-done.2), channel_id=1, replica_groups=mesh['gx'=8,'gy'=4] {'gy'}, dimensions={0}, use_global_device_ids=true | all-gather | bytes 184320 | tf_op jit(solution)/shard_map/all_gather | solution.py:106
  55.6 13.6 %all_gather.7 = f32[384,96]{1,0:T(8,128)S(1)} all-gather(f32[96,96]{1,0:T(8,128)S(1)} %copy-done.3), channel_id=1, replica_groups=mesh['gx'=8,'gy'=4] {'gy'}, dimensions={0}, use_global_device_ids=true | all-gather | bytes 184320 | tf_op jit(solution)/shard_map/all_gather | solution.py:107
  69.2 1.3 %while.30 = (s32[]{:T(128)}, f32[3,1,96,64]{2,3,0,1:T(8,128)S(1)}, f32[4,3,1,96,64]{3,4,1,2,0:T(8,128)S(1)}, f32[4,3,1,96,64]{3,4,1,2,0:T(8,128)S(1)}, f32[4,96,96]{2,1,0:T(8,128)S(1)}, /*index=5*/s32[]{:T(128)}, s32[]{:T(128)}) while((s32[]{:T(128)}, f32[3,1,96,64]{2,3,0,1:T(8,128)S(1)}, f32[4,3,1,96,64]{3,4,1,2,0:T(8,128)S(1)}, ...), condition=%wide.region_1.2_spmd.clone, body=%wide.region_0.1_spmd.clone.sunk | while | flops 21270532 | bytes 786527 | solution.py:53
  69.6 0.3 fusion.46
  69.9 0.3 fusion.46
  70.2 0.3 fusion.46
  70.6 1.3 %while.31 = (s32[]{:T(128)}, f32[3,1,96,64]{2,3,0,1:T(8,128)S(1)}, f32[4,3,1,96,64]{3,4,1,2,0:T(8,128)S(1)}, f32[4,3,1,96,64]{3,4,1,2,0:T(8,128)S(1)}, f32[4,96,...) while((s32[]{:T(128)}, f32[3,1,96,64]{2,3,0,1:T(8,128)S(1)}, ...), condition=%wide.region_3.4_spmd.clone, body=%wide.region_2.3_spmd.clone.sunk | while | flops 21270532 | bytes 786547 | solution.py:54
  70.9 0.3 fusion.49
  71.6 0.3 fusion.49
  71.9 0.3 copy.35
  72.2 0.7 reshape.122
  73.0 0.5 broadcast.111
  73.5 2.6 %reduce = f32[384,3,64]{2,1,0:T(4,128)S(1)} reduce(f32[384,3,1,1,64]{4,3,2,1,0:T(1,128)S(1)} %bitcast.125, f32[]{:T(128)} %broadcast.111), dimensions={2,3}, to_apply=%bitcast.93.reduce_sub_computation | reduce | bytes 589828
  76.1 0.6 reshape.123
  76.7 10.8 %all_to_all.30 = f32[4,1,18432]{2,1,0:T(1,128)S(1)} all-to-all(f32[4,1,18432]{2,1,0:T(1,128)S(1)} %reshape.123), channel_id=1, replica_groups=mesh['gx'=8,'gy'=4] {'gy'}, dimensions={0} | all-to-all | bytes 589824 | tf_op jit(solution)/shard_map/all_to_all | solution.py:120
  87.5 1.5 %reduce.1 = f32[4,18432]{1,0:T(4,128)S(1)} reduce(f32[4,1,18432]{2,1,0:T(1,128)S(1)} %all_to_all.30, f32[]{:T(128)} %broadcast.111), dimensions={1}, to_apply=%all_to_all.25.reduce_sub_computation | reduce | bytes 589828 | tf_op jit(solution)/shard_map/all_to_all | solution.py:120
  88.9 0.7 reshape.124
  89.7 0.8 copy.32
  90.5 0.3 all_to_all.26
  90.8 0.9 copy.34
  (46 shorter events, 2.0 us)
Async XLA Ops:
  0.0 29.9 %copy-start = (f32[96,96]{1,0:T(8,128)S(1)}, f32[96,96]{1,0:T(8,128)}, u32[]{:S(2)}) copy-start(f32[96,96]{1,0:T(8,128)} %param.9) | copy-start | bytes 110596
  0.8 1.0 %copy-start.1 = (f32[3,1,96,128]{3,2,1,0:T(8,128)S(1)}, f32[3,1,96,128]{3,2,1,0:T(8,128)}, u32[]{:S(2)}) copy-start(f32[3,1,96,128]{3,2,1,0:T(8,128)} %param.8) | copy-start | bytes 442372
  1.9 10.1 %collective-permute-start = (f32[6,1,96,128]{3,2,0,1:T(8,128)S(1)}, f32[6,1,96,128]{3,2,0,1:T(8,128)S(1)}, u32[]{:S(2)}, u32[]{:S(2)}) collective-permute-start(f32[6,1,96,128]{3,2,0,1:T(8,128)S(1)} %pad_maximum_fusion), channel_id=1, source_target_pairs={{0,16},{4,20},{8,24},{12,28},{16,0},{20,4},{24,8},{28,12},{1,17},{... | collective-permute-start | bytes 884744 | tf_op jit(solution)/shard_map/ppermute | solution.py:12
  12.1 14.6 %collective-permute-start.1 = (f32[2,6,1,96,128]{4,3,1,2,0:T(8,128)S(1)}, f32[2,6,1,96,128]{4,3,1,2,0:T(8,128)S(1)}, u32[]{:S(2)}, u32[]{:S(2)}) collective-permute-start(f32[2,6,1,96,128]{4,3,1,2,0:T(8,128)S(1)} %maximum_select_fusion), channel_id=1, source_target_pairs={{0,8},{4,12},{8,0},{12,4},{16,24},{20,28},{24,16},{28,20},{1,9},{5... | collective-permute-start | bytes 1769480 | tf_op jit(solution)/shard_map/ppermute | solution.py:12
  26.9 2.1 %collective-permute-start.2 = (f32[2,6,1,96,128]{4,3,1,2,0:T(8,128)S(1)}, f32[2,6,1,96,128]{4,3,1,2,0:T(8,128)S(1)}, u32[]{:S(2)}, u32[]{:S(2)}) collective-permute-start(f32[2,6,1,96,128]{4,3,1,2,0:T(8,128)S(1)} %maximum_select_fusion.1), channel_id=1, source_target_pairs={{0,4},{4,0},{8,12},{12,8},{16,20},{20,16},{24,28},{28,24},{1,5},{5... | collective-permute-start | bytes 1769480 | tf_op jit(solution)/shard_map/ppermute | solution.py:12
  31.2 4.9 %copy-start.2 = (f32[96,96]{1,0:T(8,128)S(1)}, f32[96,96]{1,0:T(8,128)}, u32[]{:S(2)}) copy-start(f32[96,96]{1,0:T(8,128)} %param.10) | copy-start | bytes 110596
  31.2 37.9 %all-to-all-start = ((f32[3,1,96,4,64]{2,4,0,1,3:T(8,128)}), f32[3,1,96,4,64]{2,4,0,1,3:T(8,128)S(1)}, u32[]{:S(2)}, u32[]{:S(2)}) async-start(f32[3,1,96,4,64]{2,4,0,1,3:T(8,128)} %copy.28), calls=%async_computation | async-start | bytes 786432 | tf_op jit(solution)/shard_map/all_to_all | solution.py:112
  36.2 19.4 %copy-start.3 = (f32[96,96]{1,0:T(8,128)S(1)}, f32[96,96]{1,0:T(8,128)}, u32[]{:S(2)}) copy-start(f32[96,96]{1,0:T(8,128)} %param.11) | copy-start | bytes 110596
where the time goes:
time: 92 us; the launch traced here: 91.6 us
  blocking collectives  43.8 us (48%)
  waiting for transfers between devices  21.1 us (23%)
  starting transfers between devices  9.85 us (11%)
  local copies, waits for them, and re-layouts  6.69 us (7%)
  other arithmetic  6.21 us (7%)
  matrix products  3.06 us (3%)
    ppermute x3, waiting for transfers between devices, from_partner(): lax.ppermute(shard, axis, [(i, i ^ 1 << bit) for i in range(lax.axis_size...  21.1 us
    all_gather x1, blocking collectives, shards(): lax.all_gather(lower_map, 'gy', axis=0, tiled=True)  19.4 us
    all_gather x1, blocking collectives, shards(): lax.all_gather(upper_map, 'gy', axis=0, tiled=True)  13.6 us
    all_to_all x1, blocking collectives, shards(): lax.all_to_all(whole, 'gy', split_axis=2, concat_axis=3, tiled=True)  10.8 us
    all_to_all x1, starting transfers between devices, shards(): lax.all_to_all(grouped, 'gy', split_axis=3, concat_axis=2, tiled=True)  4.94 us
    ppermute x3, starting transfers between devices, from_partner(): lax.ppermute(shard, axis, [(i, i ^ 1 << bit) for i in range(lax.axis_size...  4.91 us
    unnamed x3, other arithmetic  2.57 us
    while x8, matrix products  2.02 us
  transfers between devices with their start and end apart: 4, of which 3 were waited for; matrix products, arithmetic and copies ran while one was open for 0% of the time, Pallas kernels for 0%

commit v1 on v0

v1 whole, which is shorter than its diff:
```python
import functools
import math

import jax
import jax.numpy as jnp
from jax import lax
from jax.experimental import pallas as pl
from jax.experimental.pallas import tpu as pltpu
from jax.sharding import PartitionSpec as P

courant = 0.8
HIGHEST = lax.Precision.HIGHEST


def split(x):
    high = x.astype(jnp.bfloat16)
    return high, (x - high.astype(jnp.float32)).astype(jnp.bfloat16)


def dot3(a, b):
    dot = functools.partial(jnp.dot, preferred_element_type=jnp.float32)
    return dot(a[0], b[0]) + (dot(a[0], b[1]) + dot(a[1], b[0]))


def dot_full(a, b):
    return jnp.dot(a, b, precision=HIGHEST, preferred_element_type=jnp.float32)


def reversed_position(position, levels):
    result = position * 0
    for place in range(levels):
        result = result + ((position >> place) & 1) * (1 << (levels - 1 - place))
    return result


def kernel(
    n_gx, n_gy, chunk,
    v_ref, b_ref, l_ref, r_ref, o_ref,
    gat, coef, table, acc, g_in, g_out, stack, chain,
    d_in, d_out, u_in, u_out,
    gx_send, gx_recv, g_send, g_recv, d_send, d_recv, u_send, u_recv,
):
    items, rows, local_x = v_ref.shape
    planes = items // 3
    half = rows // 2
    levels = n_gx.bit_length() - 1
    total_x = local_x * n_gx
    me = lax.axis_index("gx")
    z = lax.axis_index("gy")
    lead = reversed_position(me, levels)
    first, last = z == 0, z == n_gy - 1

    barrier = pltpu.get_barrier_semaphore()
    for place in range(levels):
        pl.semaphore_signal(barrier, inc=1, device_id={"gx": me ^ (1 << place)}, device_id_type=pl.DeviceIdType.MESH)

    @pl.when(z > 0)
    def _():
        pl.semaphore_signal(barrier, inc=1, device_id={"gy": z - 1}, device_id_type=pl.DeviceIdType.MESH)

    @pl.when(z < n_gy - 1)
    def _():
        pl.semaphore_signal(barrier, inc=1, device_id={"gy": z + 1}, device_id_type=pl.DeviceIdType.MESH)

    peers = levels + jnp.where(z > 0, 1, 0) + jnp.where(z < n_gy - 1, 1, 0)
    pl.semaphore_wait(barrier, peers)

    outer = [1 << place for place in reversed(range(1, levels))]
    turn = len(outer) // 2
    orders = [outer + [1], outer[turn:] + outer[:turn] + [1]]
    if levels == 0:
        orders = [[], []]

    def piece(part, mask):
        span = pl.ds(part * half, half)
        return v_ref.at[:, span, :] if mask == 0 else gat.at[mask, :, span, :]

    def copy(part, mask, bit):
        return pltpu.make_async_remote_copy(
            src_ref=piece(part, mask),
            dst_ref=gat.at[mask | bit, :, pl.ds(part * half, half), :],
            send_sem=gx_send.at[part, mask | bit],
            recv_sem=gx_recv.at[part, mask | bit],
            device_id={"gx": me ^ bit},
            device_id_type=pl.DeviceIdType.MESH,
        )

    def last_bit(part, mask):
        return [bit for bit in orders[part] if mask & bit][-1]

    def forward(part, mask):
        order = orders[part]
        begin = order.index(last_bit(part, mask)) + 1 if mask else 0
        for bit in order[begin:]:
            copy(part, mask, bit).start()

    def arrive(part, mask):
        bit = last_bit(part, mask)
        copy(part, mask ^ bit, bit).wait_recv()

    for part in range(2):
        forward(part, 0)

    def g_copy():
        return pltpu.make_async_remote_copy(
            src_ref=g_out, dst_ref=g_in, send_sem=g_send, recv_sem=g_recv,
            device_id={"gy": jnp.maximum(z - 1, 0)}, device_id_type=pl.DeviceIdType.MESH,
        )

    def keep_matrices(hb):
        for ref, top, low in ((stack, b_ref[...], hb), (chain, l_ref[...], g_out[...])):
            both = split(jnp.concatenate([top, low], 0))
            ref[0], ref[1] = both

    @pl.when(last)
    def _():
        g_out[...] = l_ref[...]
        if n_gy > 1:
            g_copy().start()
        keep_matrices(b_ref[...])

    def g_step():
        g_copy().wait_recv()
        inner = dot_full(r_ref[...], g_in[...])
        g_out[...] = l_ref[...] + dot_full(inner, l_ref[...])

        @pl.when(z > 0)
        def _():
            g_copy().start()

        keep_matrices(b_ref[...] + dot_full(inner, b_ref[...]))

    masks = lax.broadcasted_iota(jnp.int32, coef.shape[1:], 0)
    turns = ((masks ^ me) * lead) & (n_gx - 1)
    angles = turns.astype(jnp.float32) * (2.0 * math.pi / n_gx)
    coef[0] = jnp.cos(angles)
    coef[1] = -jnp.sin(angles)
    cells = lax.broadcasted_iota(jnp.int32, (local_x, local_x), 0)
    waves = lead + n_gx * lax.broadcasted_iota(jnp.int32, (local_x, local_x), 1)
    phases = ((cells * waves) & (total_x - 1)).astype(jnp.float32) * (2.0 * math.pi / total_x)
    scale = 1.0 / math.sqrt(total_x)
    cosine = jnp.cos(phases) * scale
    sine = jnp.sin(phases) * scale
    signed = jnp.where(waves < total_x // 2, waves, waves - total_x)
    rate = courant * signed.astype(jnp.float32) / (total_x // 2)
    quarters = (
        (cosine, -sine), (sine, cosine),
        (-rate * sine, -rate * cosine), (rate * cosine, -rate * sine),
    )
    for i, pair in enumerate(quarters):
        for j, values in enumerate(pair):
            where = (pl.ds(i * local_x, local_x), pl.ds(j * local_x, local_x))
            high, low = split(values)
            table[(0,) + where] = high
            table[(1,) + where] = low

    def absorb(group, fresh):
        leads = [v_ref[s] if m == 0 else gat[m, s] for m in group for s in range(planes)]
        for i in range(items):
            sums = [None] * 4
            for at, m in enumerate(group):
                own = v_ref[i] if m == 0 else gat[m, i]
                flux = own * leads[at * planes + i % planes]
                c, s = coef[0, m : m + 1, :], coef[1, m : m + 1, :]
                for k, term in enumerate((own * c, own * s, flux * c, flux * s)):
                    sums[k] = term if sums[k] is None else sums[k] + term
            for k in range(4):
                lanes = pl.ds(k * local_x, local_x)
                if fresh:
                    acc[i, :, lanes] = sums[k]
                else:
                    acc[i, :, lanes] = acc[i, :, lanes] + sums[k]

    if n_gy > 1:
        pl.when(z == n_gy - 2)(g_step)
    absorb([0], True)
    by_hops = {}
    for m in range(1, n_gx):
        by_hops.setdefault(((m >> 1).bit_count(), m & 1), []).append(m)
    for at, key in enumerate(sorted(by_hops)):
        group = by_hops[key]
        for m in group:
            for part in range(2):
                arrive(part, m)
                forward(part, m)
        for begin in range(0, len(group), 2):
            absorb(group[begin : begin + 2], False)
        if n_gy > 2 and key == (1, 0):
            pl.when(z == n_gy - 3)(g_step)
    if n_gy > 3:
        pl.when(z < n_gy - 3)(g_step)

    width = 2 * local_x
    per_item = width // chunk
    count = items * per_item

    def chain_copy(down, c):
        src, dst, send, recv = (d_out, d_in, d_send, d_recv) if down else (u_out, u_in, u_send, u_recv)
        to = jnp.minimum(z + 1, n_gy - 1) if down else jnp.maximum(z - 1, 0)
        return pltpu.make_async_remote_copy(
            src_ref=src.at[c], dst_ref=dst.at[c], send_sem=send.at[c], recv_sem=recv.at[c],
            device_id={"gy": to}, device_id_type=pl.DeviceIdType.MESH,
        )

    def lanes_of(c):
        return c // per_item, pl.ds((c % per_item) * chunk, chunk)

    for i in range(items):
        side = split(dot3(split(acc[i]), (table[0], table[1])))
        both = dot3((stack[0], stack[1]), side)
        o_ref[i] = both[rows:]
        for k in range(per_item):
            c = i * per_item + k
            d_out[c] = both[:rows, k * chunk : (k + 1) * chunk]
            u_out[c] = both[rows:, k * chunk : (k + 1) * chunk]

            if n_gy > 1:
                @pl.when(first)
                def _():
                    chain_copy(True, c).start()

                @pl.when(last)
                def _():
                    chain_copy(False, c).start()

    def step_down(c):
        i, lanes = lanes_of(c)

        @pl.when(z > 0)
        def _():
            chain_copy(True, c).wait_recv()
            got = dot3((chain[0], chain[1]), split(d_in[c]))

            @pl.when(z < n_gy - 1)
            def _():
                d_out[c] = d_out[c] + got[:rows]
                chain_copy(True, c).start()

            o_ref[i, :, lanes] = o_ref[i, :, lanes] + got[rows:]

    upper = split(r_ref[...])

    def step_up(c):
        i, lanes = lanes_of(c)

        @pl.when(z < n_gy - 1)
        def _():
            chain_copy(False, c).wait_recv()
            got = dot3(upper, split(u_in[c]))

            @pl.when(z > 0)
            def _():
                u_out[c] = u_out[c] + got
                chain_copy(False, c).start()

            o_ref[i, :, lanes] = o_ref[i, :, lanes] + got

    lag = min(3, count)
    if n_gy > 1:
        for early, late, here in (
            (step_down, step_up, z < n_gy // 2),
            (step_up, step_down, z >= n_gy // 2),
        ):
            @pl.when(here)
            def _():
                for s in range(count + lag):
                    if s < count:
                        early(s)
                    if s >= lag:
                        late(s - lag)

    for part in range(2):
        for m in range(1, n_gx):
            bit = last_bit(part, m)
            copy(part, m ^ bit, bit).wait_send()
    if n_gy > 1:
        @pl.when(z > 0)
        def _():
            g_copy().wait_send()
            for c in range(count):
                chain_copy(False, c).wait_send()

        @pl.when(z < n_gy - 1)
        def _():
            for c in range(count):
                chain_copy(True, c).wait_send()


def shards(velocity, block_inverse, lower_map, upper_map):
    comps, planes, rows, local_x = velocity.shape
    n_gx, n_gy = lax.axis_size("gx"), lax.axis_size("gy")
    items = comps * planes
    chunk = local_x
    count = items * 2 * local_x // chunk
    f32, bf16 = jnp.float32, jnp.bfloat16
    vmem, dma = pltpu.VMEM, pltpu.SemaphoreType.DMA
    out = pl.pallas_call(
        functools.partial(kernel, n_gx, n_gy, chunk),
        out_shape=jax.ShapeDtypeStruct((items, rows, 2 * local_x), f32),
        in_specs=[pl.BlockSpec(memory_space=pltpu.VMEM)] * 4,
        out_specs=pl.BlockSpec(memory_space=pltpu.VMEM),
        scratch_shapes=[
            vmem((n_gx, items, rows, local_x), f32),
            vmem((2, max(n_gx, 8), local_x), f32),
            vmem((2, 4 * local_x, 2 * local_x), bf16),
            vmem((items, rows, 4 * local_x), f32),
            vmem((rows, rows), f32),
            vmem((rows, rows), f32),
            vmem((2, 2 * rows, rows), bf16),
            vmem((2, 2 * rows, rows), bf16),
            vmem((count, rows, chunk), f32),
            vmem((count, rows, chunk), f32),
            vmem((count, rows, chunk), f32),
            vmem((count, rows, chunk), f32),
            dma((2, n_gx)), dma((2, n_gx)), dma, dma,
            dma((count,)), dma((count,)), dma((count,)), dma((count,)),
        ],
        compiler_params=pltpu.CompilerParams(
            collective_id=0, has_side_effects=True, vmem_limit_bytes=48 * 2**20
        ),
        name="step",
    )(velocity.reshape(items, rows, local_x), block_inverse, lower_map, upper_map)
    return out.reshape(comps, planes, rows, 2 * local_x)


def solution(mesh):
    return jax.shard_map(
        shards,
        mesh=mesh,
        in_specs=(P(None, None, "gy", "gx"), P("gy", None), P("gy", None), P("gy", None)),
        out_specs=P(None, None, "gy", "gx"),
        check_vma=False,
    )
```

time: 92 us -> 35.7 us (0.39)
  blocking collectives: 43.8 us -> 0 us
  Pallas kernels: 0 us -> 31.4 us
  waiting for transfers between devices: 21.1 us -> 0 us
  starting transfers between devices: 9.85 us -> 0 us
  other arithmetic: 6.21 us -> 0 us
  matrix products: 3.06 us -> 0 us
  local copies, waits for them, and re-layouts: 6.69 us -> 4.02 us
    all_gather x2 -> x0, blocking collectives: 33 us -> none  [the longest x1 19.4 us: shards(): lax.all_gather(lower_map, 'gy', axis=0, tiled=True)]
    pallas_call x0 -> x1, Pallas kernels: none -> 31.4 us  [shards(): pl.pallas_call(functools.partial(kernel, n_gx, n_gy, chunk), out_shape=ja...]
    ppermute x3 -> x0, waiting for transfers between devices: 21.1 us -> none  [from_partner(): lax.ppermute(shard, axis, [(i, i ^ 1 << bit) for i in range(lax.axis_size...]
    all_to_all x1 -> x0, blocking collectives: 10.8 us -> none  [shards(): lax.all_to_all(whole, 'gy', split_axis=2, concat_axis=3, tiled=True)]
    all_to_all x1 -> x0, starting transfers between devices: 4.94 us -> none  [shards(): lax.all_to_all(grouped, 'gy', split_axis=3, concat_axis=2, tiled=True)]
    ppermute x3 -> x0, starting transfers between devices: 4.91 us -> none  [from_partner(): lax.ppermute(shard, axis, [(i, i ^ 1 << bit) for i in range(lax.axis_size...]
    reshape x4 -> x0, local copies, waits for them, and re-layouts: 2.71 us -> none  [the longest x2 1.06 us: shards(): jnp.moveaxis(solved_blocks, 0, 2)]
    unnamed x3 -> x0, other arithmetic: 2.57 us -> none
  transfers between devices with their start and end apart: 4 -> 0, of which waited for: 3 -> 0; matrix products, arithmetic and copies ran while one was open for 0% -> 0% of each run, Pallas kernels for 0% -> 0%
where the time goes in v1:
time: 35.7 us; the launch traced here: 35.4 us
  Pallas kernels  31.4 us (88%)
  local copies, waits for them, and re-layouts  4.02 us (11%)
    pallas_call x1, Pallas kernels, shards(): pl.pallas_call(functools.partial(kernel, n_gx, n_gy, chunk), out_shape=ja...  31.4 us
    unnamed x9, local copies, waits for them, and re-layouts  4.02 us

profile of v1, /device:TPU:0, one launch (start us, length us, event | category | flops | bytes accessed | tf_op | source)
XLA Modules:
  0.0 35.4 jit_solution(4394047476238734826)
XLA Ops:
  0.0 0.0 copy-start
  0.0 0.9 %copy-done = f32[3,1,96,128]{3,2,1,0:T(8,128)S(1)} copy-done((f32[3,1,96,128]{3,2,1,0:T(8,128)S(1)}, f32[3,1,96,128]{3,2,1,0:T(8,128)}, u32[]{:S(2)}) %copy-start) | copy-done | bytes 147480
  0.9 0.0 copy-start.1
  0.9 0.8 %copy-done.1 = f32[96,96]{1,0:T(8,128)S(1)} copy-done((f32[96,96]{1,0:T(8,128)S(1)}, f32[96,96]{1,0:T(8,128)}, u32[]{:S(2)}) %copy-start.1) | copy-done | bytes 36888
  1.7 0.0 copy-start.2
  1.7 0.8 %copy-done.2 = f32[96,96]{1,0:T(8,128)S(1)} copy-done((f32[96,96]{1,0:T(8,128)S(1)}, f32[96,96]{1,0:T(8,128)}, u32[]{:S(2)}) %copy-start.2) | copy-done | bytes 36888
  2.5 0.0 copy-start.3
  2.5 0.8 %copy-done.3 = f32[96,96]{1,0:T(8,128)S(1)} copy-done((f32[96,96]{1,0:T(8,128)S(1)}, f32[96,96]{1,0:T(8,128)}, u32[]{:S(2)}) %copy-start.3) | copy-done | bytes 36888
  3.3 31.4 %step.1 = f32[3,96,256]{2,1,0:T(8,128)S(1)} custom-call(f32[3,96,128]{2,1,0:T(8,128)S(1)} %bitcast.5, f32[96,96]{1,0:T(8,128)S(1)} %copy-done.1, f32[96,96]{1,0:T(8,128)S(1)} %copy-done.2, f32[96,96]{1,0:T(8,128)S(1)} %copy-done.3), custom_call_target="tpu_custom_call" | custom-call | tf_op jit(solution)/shard_map/step/pallas_call | solution.py:297
  34.7 0.7 %copy.7 = f32[3,1,96,256]{3,2,1,0:T(8,128)} copy(f32[3,1,96,256]{3,2,1,0:T(8,128)S(1)} %bitcast.4) | data formatting | bytes 589824
Async XLA Ops:
  0.0 0.9 %copy-start = (f32[3,1,96,128]{3,2,1,0:T(8,128)S(1)}, f32[3,1,96,128]{3,2,1,0:T(8,128)}, u32[]{:S(2)}) copy-start(f32[3,1,96,128]{3,2,1,0:T(8,128)} %param.4) | copy-start | bytes 442372
  0.9 0.8 %copy-start.1 = (f32[96,96]{1,0:T(8,128)S(1)}, f32[96,96]{1,0:T(8,128)}, u32[]{:S(2)}) copy-start(f32[96,96]{1,0:T(8,128)} %b_ref.1) | copy-start | bytes 110596
  1.7 0.8 %copy-start.2 = (f32[96,96]{1,0:T(8,128)S(1)}, f32[96,96]{1,0:T(8,128)}, u32[]{:S(2)}) copy-start(f32[96,96]{1,0:T(8,128)} %l_ref.1) | copy-start | bytes 110596
  2.5 0.8 %copy-start.3 = (f32[96,96]{1,0:T(8,128)S(1)}, f32[96,96]{1,0:T(8,128)}, u32[]{:S(2)}) copy-start(f32[96,96]{1,0:T(8,128)} %r_ref.1) | copy-start | bytes 110596

commit v2 on v1

v2 whole, which is shorter than its diff:
```python
import functools
import math

import jax
import jax.numpy as jnp
from jax import lax
from jax.experimental import pallas as pl
from jax.experimental.pallas import tpu as pltpu
from jax.sharding import PartitionSpec as P

courant = 0.8


def split(x):
    high = x.astype(jnp.bfloat16)
    return high, (x - high.astype(jnp.float32)).astype(jnp.bfloat16)


def dot3(a, b):
    dot = functools.partial(jnp.dot, preferred_element_type=jnp.float32)
    return dot(a[0], b[0]) + (dot(a[0], b[1]) + dot(a[1], b[0]))


def reversed_position(position, levels):
    result = position * 0
    for place in range(levels):
        result = result + ((position >> place) & 1) * (1 << (levels - 1 - place))
    return result


def kernel(
    n_gx, n_gy, chunk,
    v_hbm, b_hbm, l_hbm, r_hbm, o_ref,
    v_ref, b_ref, l_ref, r_ref, gat, coef, table, acc, g_in, g_out,
    d_in, d_out, u_in, u_out, across,
    own_sem, map_sem, gx_send, gx_recv, g_send, g_recv, d_send, d_recv, u_send, u_recv,
):
    items, rows, local_x = v_ref.shape
    planes = items // 3
    half = rows // 2
    levels = n_gx.bit_length() - 1
    hops = max(levels - 1, 0)
    total_x = local_x * n_gx
    me = lax.axis_index("gx")
    z = lax.axis_index("gy")
    lead = reversed_position(me, levels)
    first, last = z == 0, z == n_gy - 1
    mesh_type = pl.DeviceIdType.MESH

    own = [pltpu.make_async_copy(v_hbm.at[i], v_ref.at[i], own_sem.at[i]) for i in range(items)]
    maps = [
        pltpu.make_async_copy(src, dst, map_sem.at[i])
        for i, (src, dst) in enumerate(((l_hbm, l_ref), (r_hbm, r_ref), (b_hbm, b_ref)))
    ]
    for local in own + maps:
        local.start()

    barrier = pltpu.get_barrier_semaphore()
    for place in range(levels):
        pl.semaphore_signal(barrier, inc=1, device_id={"gx": me ^ (1 << place)}, device_id_type=mesh_type)

    @pl.when(z > 0)
    def _():
        pl.semaphore_signal(barrier, inc=1, device_id={"gy": z - 1}, device_id_type=mesh_type)

    @pl.when(z < n_gy - 1)
    def _():
        pl.semaphore_signal(barrier, inc=1, device_id={"gy": z + 1}, device_id_type=mesh_type)

    for local in own + maps:
        local.wait()
    peers = levels + jnp.where(z > 0, 1, 0) + jnp.where(z < n_gy - 1, 1, 0)
    pl.semaphore_wait(barrier, peers)

    outer = [1 << place for place in reversed(range(1, levels))]
    turn = len(outer) // 2
    orders = [outer + [1], outer[turn:] + outer[:turn] + [1]]

    def copy(item, part, mask, bit):
        span = pl.ds(part * half, half)
        return pltpu.make_async_remote_copy(
            src_ref=gat.at[mask, item, span, :] if mask else v_ref.at[item, span, :],
            dst_ref=gat.at[mask | bit, item, span, :],
            send_sem=gx_send.at[item, part, mask | bit],
            recv_sem=gx_recv.at[item, part, mask | bit],
            device_id={"gx": me ^ bit},
            device_id_type=mesh_type,
        )

    def last_bit(part, mask):
        return [bit for bit in orders[part] if mask & bit][-1]

    def arrive(item, part, mask):
        bit = last_bit(part, mask)
        copy(item, part, mask ^ bit, bit).wait_recv()

    def forward(item, masks):
        for mask in masks:
            begins = []
            for part in range(2):
                if mask:
                    arrive(item, part, mask)
                begins.append(orders[part].index(last_bit(part, mask)) + 1 if mask else 0)
            for at in range(len(orders[0])):
                for part in range(2):
                    if at >= begins[part]:
                        copy(item, part, mask, orders[part][at]).start()

    if n_gx > 1:
        for item in range(items if hops == 0 else min(2, items)):
            forward(item, [0])

    def g_copy():
        return pltpu.make_async_remote_copy(
            src_ref=g_out, dst_ref=g_in, send_sem=g_send, recv_sem=g_recv,
            device_id={"gy": jnp.maximum(z - 1, 0)}, device_id_type=mesh_type,
        )

    if n_gy > 1:
        @pl.when(last)
        def _():
            g_out[...] = l_ref[...]
            g_copy().start()

    def g_step():
        g_copy().wait_recv()

        @pl.when(z > 0)
        def _():
            low = l_ref[...]
            inner = dot3(split(g_in[...]), split(low))
            g_out[...] = low + dot3(split(r_ref[...]), split(inner))
            g_copy().start()

    masks = lax.broadcasted_iota(jnp.int32, coef.shape[1:], 0)
    turns = ((masks ^ me) * lead) & (n_gx - 1)
    angles = turns.astype(jnp.float32) * (2.0 * math.pi / n_gx)
    coef[0] = jnp.cos(angles)
    coef[1] = -jnp.sin(angles)
    cells = lax.broadcasted_iota(jnp.int32, (local_x, local_x), 0)
    waves = lead + n_gx * lax.broadcasted_iota(jnp.int32, (local_x, local_x), 1)
    phases = ((cells * waves) & (total_x - 1)).astype(jnp.float32) * (2.0 * math.pi / total_x)
    scale = 1.0 / math.sqrt(total_x)
    cosine = jnp.cos(phases) * scale
    sine = jnp.sin(phases) * scale
    signed = jnp.where(waves < total_x // 2, waves, waves - total_x)
    rate = courant * signed.astype(jnp.float32) / (total_x // 2)
    quarters = (
        (cosine, -sine), (sine, cosine),
        (-rate * sine, -rate * cosine), (rate * cosine, -rate * sine),
    )
    for i, pair in enumerate(quarters):
        for j, values in enumerate(pair):
            where = (pl.ds(i * local_x, local_x), pl.ds(j * local_x, local_x))
            high, low = split(values)
            table[(0,) + where] = high
            table[(1,) + where] = low

    def absorb(i, group, fresh):
        for begin in range(0, len(group), 4):
            sums = [None] * 4
            for m in group[begin : begin + 4]:
                mine = gat[m, i] if m else v_ref[i]
                flux = mine * (gat[m, i % planes] if m else v_ref[i % planes])
                c, s = coef[0, m : m + 1, :], coef[1, m : m + 1, :]
                for k, term in enumerate((mine * c, mine * s, flux * c, flux * s)):
                    sums[k] = term if sums[k] is None else sums[k] + term
            for k in range(4):
                lanes = pl.ds(k * local_x, local_x)
                acc[i, :, lanes] = sums[k] if fresh and begin == 0 else acc[i, :, lanes] + sums[k]

    width = 2 * local_x
    per_item = width // chunk
    count = items * per_item

    def chain_copy(down, c):
        src, dst, send, recv = (d_out, d_in, d_send, d_recv) if down else (u_out, u_in, u_send, u_recv)
        to = jnp.minimum(z + 1, n_gy - 1) if down else jnp.maximum(z - 1, 0)
        return pltpu.make_async_remote_copy(
            src_ref=src.at[c], dst_ref=dst.at[c], send_sem=send.at[c], recv_sem=recv.at[c],
            device_id={"gy": to}, device_id_type=mesh_type,
        )

    def lanes_of(c):
        return c // per_item, pl.ds((c % per_item) * chunk, chunk)

    def finish(i):
        side = split(dot3(split(acc[i]), (table[0], table[1])))
        load = dot3(split(b_ref[...]), side)
        o_ref[i] = load
        for k in range(per_item):
            c = i * per_item + k
            d_out[c] = load[:, k * chunk : (k + 1) * chunk]
            u_out[c] = load[:, k * chunk : (k + 1) * chunk]

            if n_gy > 1:
                @pl.when(first)
                def _():
                    chain_copy(True, c).start()

                @pl.when(last)
                def _():
                    chain_copy(False, c).start()

    level_of = [[m for m in range(0, n_gx, 2) if m.bit_count() == h] for h in range(hops + 1)]
    events = sorted((2 * h + i, i, h) for h in range(1, hops + 1) for i in range(items))

    def complete(i):
        odd = [m | 1 for m in level_of[hops] if m | 1 < n_gx]
        for m in odd:
            for part in range(2):
                arrive(i, part, m)
        group = odd + ([0] if hops == 0 else [])
        absorb(i, group, hops == 0)
        finish(i)

    ready = []
    for at, (slot, i, h) in enumerate(events):
        forward(i, level_of[h])
        if h == 1 and i + 2 < items:
            forward(i + 2, [0])
        odd = [m | 1 for m in level_of[h - 1]]
        for m in odd:
            for part in range(2):
                arrive(i, part, m)
        absorb(i, ([0] if h == 1 else []) + odd + level_of[h], h == 1)
        if n_gy > 1 and at == min(1, len(events) - 1):
            pl.when(z == n_gy - 2)(g_step)
        for done in ready:
            complete(done)
        ready = [i] if h == hops else []
    if n_gy > 1 and not events:
        pl.when(z == n_gy - 2)(g_step)
    for done in ready if events else range(items):
        complete(done)

    def step_down(c):
        i, lanes = lanes_of(c)

        @pl.when(z > 0)
        def _():
            chain_copy(True, c).wait_recv()
            got = dot3(lower, split(d_in[c]))

            @pl.when(z < n_gy - 1)
            def _():
                d_out[c] = d_out[c] + got[:rows]
                chain_copy(True, c).start()

            o_ref[i, :, lanes] = o_ref[i, :, lanes] + got[rows:]

    def step_up(c):
        i, lanes = lanes_of(c)

        @pl.when(z < n_gy - 1)
        def _():
            chain_copy(False, c).wait_recv()
            got = dot3(upper, split(across[c] + u_in[c]))

            @pl.when(z > 0)
            def _():
                u_out[c] = u_out[c] + got
                chain_copy(False, c).start()

            o_ref[i, :, lanes] = o_ref[i, :, lanes] + got

    if n_gy > 1:
        if n_gy > 2:
            pl.when(z < n_gy - 2)(g_step)

        @pl.when(z < n_gy - 1)
        def _():
            below = split(g_in[...])
            for i in range(items):
                moved = dot3(below, split(o_ref[i]))
                for k in range(per_item):
                    across[i * per_item + k] = moved[:, k * chunk : (k + 1) * chunk]

        lag = min(3, count)
        upper = split(r_ref[...])

        @pl.when(first)
        def _():
            g_out[...] = jnp.zeros_like(g_out)

        lower = split(jnp.concatenate([l_ref[...], g_out[...]], 0))
        for early, late, here in (
            (step_down, step_up, z < n_gy // 2),
            (step_up, step_down, z >= n_gy // 2),
        ):
            @pl.when(here)
            def _():
                for s in range(count + lag):
                    if s < count:
                        early(s)
                    if s >= lag:
                        late(s - lag)

    for item in range(items):
        for part in range(2):
            for m in range(1, n_gx):
                bit = last_bit(part, m)
                copy(item, part, m ^ bit, bit).wait_send()
    if n_gy > 1:
        @pl.when(z > 0)
        def _():
            g_copy().wait_send()
            for c in range(count):
                chain_copy(False, c).wait_send()

        @pl.when(z < n_gy - 1)
        def _():
            for c in range(count):
                chain_copy(True, c).wait_send()


def shards(velocity, block_inverse, lower_map, upper_map):
    comps, planes, rows, local_x = velocity.shape
    n_gx, n_gy = lax.axis_size("gx"), lax.axis_size("gy")
    items = comps * planes
    chunk = local_x
    count = items * 2 * local_x // chunk
    f32, bf16 = jnp.float32, jnp.bfloat16
    vmem, dma = pltpu.VMEM, pltpu.SemaphoreType.DMA
    out = pl.pallas_call(
        functools.partial(kernel, n_gx, n_gy, chunk),
        out_shape=jax.ShapeDtypeStruct((items, rows, 2 * local_x), f32),
        in_specs=[pl.BlockSpec(memory_space=pl.ANY)] * 4,
        out_specs=pl.BlockSpec(memory_space=pltpu.VMEM),
        scratch_shapes=[
            vmem((items, rows, local_x), f32),
            vmem((rows, rows), f32),
            vmem((rows, rows), f32),
            vmem((rows, rows), f32),
            vmem((n_gx, items, rows, local_x), f32),
            vmem((2, max(n_gx, 8), local_x), f32),
            vmem((2, 4 * local_x, 2 * local_x), bf16),
            vmem((items, rows, 4 * local_x), f32),
            vmem((rows, rows), f32),
            vmem((rows, rows), f32),
            vmem((count, rows, chunk), f32),
            vmem((count, rows, chunk), f32),
            vmem((count, rows, chunk), f32),
            vmem((count, rows, chunk), f32),
            vmem((count, rows, chunk), f32),
            dma((items,)), dma((3,)),
            dma((items, 2, n_gx)), dma((items, 2, n_gx)), dma, dma,
            dma((count,)), dma((count,)), dma((count,)), dma((count,)),
        ],
        compiler_params=pltpu.CompilerParams(
            collective_id=0, has_side_effects=True, vmem_limit_bytes=67043328
        ),
        name="step",
    )(velocity.reshape(items, rows, local_x), block_inverse, lower_map, upper_map)
    return out.reshape(comps, planes, rows, 2 * local_x)


def solution(mesh):
    return jax.shard_map(
        shards,
        mesh=mesh,
        in_specs=(P(None, None, "gy", "gx"), P("gy", None), P("gy", None), P("gy", None)),
        out_specs=P(None, None, "gy", "gx"),
        check_vma=False,
    )
```

time: 35.7 us -> 31.9 us (0.89)
  local copies, waits for them, and re-layouts: 4.02 us -> 1.69 us
  Pallas kernels: 31.4 us -> 30 us
    unnamed x9 -> x1, local copies, waits for them, and re-layouts: 4.02 us -> 1.69 us
    pallas_call x1, Pallas kernels: 31.4 us -> 30 us  [shards(): pl.pallas_call(functools.partial(kernel, n_gx, n_gy, chunk), out_shape=ja...]
where the time goes in v2:
time: 31.9 us; the launch traced here: 31.7 us
  Pallas kernels  30 us (94%)
  local copies, waits for them, and re-layouts  1.69 us (5%)
    pallas_call x1, Pallas kernels, shards(): pl.pallas_call(functools.partial(kernel, n_gx, n_gy, chunk), out_shape=ja...  30 us
    unnamed x1, local copies, waits for them, and re-layouts  1.69 us

profile of v2, /device:TPU:0, one launch (start us, length us, event | category | flops | bytes accessed | tf_op | source)
XLA Modules:
  0.0 31.7 jit_solution(10536294574399083655)
XLA Ops:
  0.0 30.0 %step.1 = f32[3,96,256]{2,1,0:T(8,128)} custom-call(f32[3,96,128]{2,1,0:T(8,128)} %bitcast.5, f32[96,96]{1,0:T(8,128)} %b_hbm.1, f32[96,96]{1,0:T(8,128)} %l_hbm.1, f32[96,96]{1,0:T(8,128)} %r_hbm.1), custom_call_target="tpu_custom_call" | custom-call | tf_op jit(solution)/shard_map/step/pallas_call | solution.py:325
  30.0 1.7 %copy.7 = f32[3,1,96,256]{3,2,1,0:T(8,128)} copy(f32[3,1,96,256]{3,2,1,0:T(8,128)} %bitcast.4) | data formatting | bytes 589824

commit v3 on v2

--- a/solution.py
+++ b/solution.py
@@ -95,20 +95,21 @@
         copy(item, part, mask ^ bit, bit).wait_recv()
 
     def forward(item, masks):
-        for mask in masks:
-            begins = []
+        pieces = [(orders[part].index(last_bit(part, m)), part, m) for m in masks for part in range(2)]
+        for place, part, mask in sorted(pieces):
+            arrive(item, part, mask)
+            for bit in orders[part][place + 1 :]:
+                copy(item, part, mask, bit).start()
+
+    def send_own(item, places):
+        for place in places:
             for part in range(2):
-                if mask:
-                    arrive(item, part, mask)
-                begins.append(orders[part].index(last_bit(part, mask)) + 1 if mask else 0)
-            for at in range(len(orders[0])):
-                for part in range(2):
-                    if at >= begins[part]:
-                        copy(item, part, mask, orders[part][at]).start()
+                copy(item, part, 0, orders[part][place]).start()
 
     if n_gx > 1:
-        for item in range(items if hops == 0 else min(2, items)):
-            forward(item, [0])
+        for item in range(items):
+            late = item >= 2 and hops > 0
+            send_own(item, range(1) if late else range(levels))
 
     def g_copy():
         return pltpu.make_async_remote_copy(
@@ -218,7 +219,7 @@
     for at, (slot, i, h) in enumerate(events):
         forward(i, level_of[h])
         if h == 1 and i + 2 < items:
-            forward(i + 2, [0])
+            send_own(i + 2, range(1, levels))
         odd = [m | 1 for m in level_of[h - 1]]
         for m in odd:
             for part in range(2):

time: 31.9 us -> 31.5 us (0.987)
  Pallas kernels: 30 us -> 29.6 us
    pallas_call x1, Pallas kernels: 30 us -> 29.6 us  [shards(): pl.pallas_call(functools.partial(kernel, n_gx, n_gy, chunk), out_shape=ja...]
where the time goes in v3:
time: 31.5 us; the launch traced here: 31.3 us
  Pallas kernels  29.6 us (94%)
  local copies, waits for them, and re-layouts  1.69 us (5%)
    pallas_call x1, Pallas kernels, shards(): pl.pallas_call(functools.partial(kernel, n_gx, n_gy, chunk), out_shape=ja...  29.6 us
    unnamed x1, local copies, waits for them, and re-layouts  1.69 us

profile of v3, /device:TPU:0, one launch (start us, length us, event | category | flops | bytes accessed | tf_op | source)
XLA Modules:
  0.0 31.3 jit_solution(12732997000474856791)
XLA Ops:
  0.0 29.6 %step.1 = f32[3,96,256]{2,1,0:T(8,128)} custom-call(f32[3,96,128]{2,1,0:T(8,128)} %bitcast.5, f32[96,96]{1,0:T(8,128)} %b_hbm.1, f32[96,96]{1,0:T(8,128)} %l_hbm.1, f32[96,96]{1,0:T(8,128)} %r_hbm.1), custom_call_target="tpu_custom_call" | custom-call | tf_op jit(solution)/shard_map/step/pallas_call | solution.py:326
  29.6 1.7 %copy.7 = f32[3,1,96,256]{3,2,1,0:T(8,128)} copy(f32[3,1,96,256]{3,2,1,0:T(8,128)} %bitcast.4) | data formatting | bytes 589824

commit v4 on v3

--- a/solution.py
+++ b/solution.py
@@ -325,7 +325,7 @@
     vmem, dma = pltpu.VMEM, pltpu.SemaphoreType.DMA
     out = pl.pallas_call(
         functools.partial(kernel, n_gx, n_gy, chunk),
-        out_shape=jax.ShapeDtypeStruct((items, rows, 2 * local_x), f32),
+        out_shape=vmem((items, rows, 2 * local_x), f32),
         in_specs=[pl.BlockSpec(memory_space=pl.ANY)] * 4,
         out_specs=pl.BlockSpec(memory_space=pltpu.VMEM),
         scratch_shapes=[
@@ -349,7 +349,7 @@
             dma((count,)), dma((count,)), dma((count,)), dma((count,)),
         ],
         compiler_params=pltpu.CompilerParams(
-            collective_id=0, has_side_effects=True, vmem_limit_bytes=67043328
+            collective_id=0, has_side_effects=True, vmem_limit_bytes=67108864 - 1000 * 1024
         ),
         name="step",
     )(velocity.reshape(items, rows, local_x), block_inverse, lower_map, upper_map)

time: 31.5 us -> 29.8 us (0.946)
  local copies, waits for them, and re-layouts: 1.69 us -> 0.72 us
  Pallas kernels: 29.6 us -> 28.9 us
    unnamed x1, local copies, waits for them, and re-layouts: 1.69 us -> 0.72 us
    pallas_call x1, Pallas kernels: 29.6 us -> 28.9 us  [shards(): pl.pallas_call(functools.partial(kernel, n_gx, n_gy, chunk), out_shape=vm...]
where the time goes in v4:
time: 29.8 us; the launch traced here: 29.6 us
  Pallas kernels  28.9 us (97%)
  local copies, waits for them, and re-layouts  0.72 us (2%)
    pallas_call x1, Pallas kernels, shards(): pl.pallas_call(functools.partial(kernel, n_gx, n_gy, chunk), out_shape=vm...  28.9 us
    unnamed x1, local copies, waits for them, and re-layouts  0.72 us

profile of v4, /device:TPU:0, one launch (start us, length us, event | category | flops | bytes accessed | tf_op | source)
XLA Modules:
  0.0 29.6 jit_solution(5889568627718806093)
XLA Ops:
  0.0 28.9 %step.1 = f32[3,96,256]{2,1,0:T(8,128)S(1)} custom-call(f32[3,96,128]{2,1,0:T(8,128)} %bitcast.5, f32[96,96]{1,0:T(8,128)} %b_hbm.1, f32[96,96]{1,0:T(8,128)} %l_hbm.1, f32[96,96]{1,0:T(8,128)} %r_hbm.1), custom_call_target="tpu_custom_call" | custom-call | tf_op jit(solution)/shard_map/step/pallas_call | solution.py:326
  28.9 0.7 %copy.7 = f32[3,1,96,256]{3,2,1,0:T(8,128)} copy(f32[3,1,96,256]{3,2,1,0:T(8,128)S(1)} %bitcast.4) | data formatting | bytes 589824
